TPU v7x, 32 devices: a whole 2x2x4 slice. The times are simulated.
32 devices in a mesh: group: 16 (over z, y, core), tp: 2 (over x).
Axes of the slice: x: 2, y: 2, z: 4, core: 2. Of those that a mesh axis runs over, the one named last changes fastest.
Arguments:
- tokens: bfloat16 [8192, 3200], P('group', 'tp'), may hold values from -6 to 6
- norm_gain: bfloat16 [3200], P('tp'), may hold values from 0.25 to 1.75
- w_qkv: bfloat16 [3200, 3, 2048], P('group', None, 'tp'), may hold values from -1 to 1, as said below
- qk_gain: float32 [2, 2048], P(None, 'tp'), may hold values from 0.5 to 8
- w_out: bfloat16 [2048, 3200], P('tp', 'group'), may hold values from -0.125 to 0.125
- layer_scale: float32 [3200], P('tp'), may hold values from 0.3 to 1.5
- request: int32 [8192], P('group'), may hold values from 0 to 8191, as said below
- owner: int32 [8192, 1], P('group'), may hold values from 0 to 15; in each aligned block of 512 rows (0 to 511, 512 to 1023, ...) at most 64 rows name the same one
Outputs:
- routed: bfloat16 [16, 16, 64, 3200], P('group', None, None, 'tp')
Inputs may be any that keep to these rules, and one draw needn't show every extreme that they name: Requests never cross a block of 1024 rows starting at a multiple of 1024, and blocks share none; in each such block exactly one request holds rows on both sides of its middle, at most 128 on each side, exactly 128 on each side in the first block; the first row's number is 0 and the last row's is 8191. Among one group's 512 rows at most 64 name the same owner; some owner is named by exactly 64 rows of some group. `w_qkv`: column scales of the projections vary across the columns.
All inputs are finite; a program needn't handle non-finite values.
Results may differ from a plain program's by a relative error of at most 0.0117.
The roundings to bfloat16 on the way count: a program that leaves them out, or rounds other values in their place, can miss the bound.
Values may be sent and summed in bfloat16 or wider, within the bound.
A program may use at most 128 MiB of HBM per device.

v0:
```python
import math
import jax
import jax.numpy as jnp
from jax import lax
from jax.sharding import PartitionSpec as P

HD = 128
SHARE = 128


def swapped(value, axis, apart):
    mask = 2**apart
    pairs = [(source, source ^ mask) for source in range(lax.axis_size(axis))]
    return lax.ppermute(value, axis, pairs)


def from_next(value, axis):
    count = lax.axis_size(axis)
    return lax.ppermute(value, axis, [((i + 1) % count, i) for i in range(count)])


def shards(tokens, norm_gain, w_qkv, qk_gain, w_out, layer_scale, request, owner):
    rows, feat_local = tokens.shape
    tp_count = lax.axis_size("tp")
    group_count = lax.axis_size("group")
    local_width = w_qkv.shape[2]
    head_count = local_width // HD
    me_tp = lax.axis_index("tp")
    w_k, w_q = (lax.all_gather(w_qkv[:, i, :], "group", axis=0, tiled=True) for i in (1, 0))
    whole = jnp.zeros((rows, feat_local * tp_count), jnp.bfloat16)
    gain_all = jnp.zeros((1, feat_local * tp_count), jnp.bfloat16)
    piece, gain = (tokens, norm_gain.reshape(1, feat_local))
    for step in range(tp_count):
        at = (me_tp + step) % tp_count * feat_local
        whole = lax.dynamic_update_slice(whole, piece, (0, at))
        gain_all = lax.dynamic_update_slice(gain_all, gain, (0, at))
        if step < tp_count - 1:
            piece, gain = (from_next(piece, "tp"), from_next(gain, "tp"))
    whole, late_v, late_out = lax.optimization_barrier((whole, w_qkv[:, 2, :], w_out))
    w_v = lax.all_gather(late_v, "group", axis=0, tiled=True)
    per = group_count // tp_count
    pairs = []
    for g in range(group_count):
        for b in range(tp_count):
            t, j = (g // per, g % per)
            to_g = (b - t) % tp_count * per + j
            pairs.append((g * tp_count + b, to_g * tp_count + t))
    w_piece = lax.ppermute(late_out.T, ("group", "tp"), pairs)
    w_o = lax.all_gather(w_piece, "group", axis=0, tiled=True)
    w_o = w_o.reshape(tp_count, feat_local, local_width)
    xwide = whole.astype(jnp.float32)
    stat = jnp.mean(xwide * xwide, axis=-1, keepdims=True)
    normed = (xwide * lax.rsqrt(stat + 1e-06) * gain_all.astype(jnp.float32)).astype(jnp.bfloat16)
    key_rows = jnp.dot(normed, w_k, preferred_element_type=jnp.float32)
    query = jnp.dot(normed, w_q, preferred_element_type=jnp.float32)
    qsum, ksum = lax.psum(
        (jnp.sum(query * query, axis=-1), jnp.sum(key_rows * key_rows, axis=-1)), "tp"
    )
    total_width = local_width * tp_count
    qnorm = (query * lax.rsqrt(qsum / total_width + 1e-06)[:, None] * qk_gain[0]).astype(
        jnp.bfloat16
    )
    knorm = (key_rows * lax.rsqrt(ksum / total_width + 1e-06)[:, None] * qk_gain[1]).astype(
        jnp.bfloat16
    )
    parity = lax.axis_index("group") % 2
    seam = jnp.where(parity == 0, rows - SHARE, 0).astype(jnp.int32)
    key_window = lax.dynamic_slice_in_dim(knorm, seam, SHARE, 0)
    id_window = lax.dynamic_slice_in_dim(request, seam, SHARE, 0)
    paired_key, paired_ids = swapped((key_window, id_window), "group", 0)
    all_keys = jnp.concatenate([knorm, paired_key], axis=0)
    all_ids = jnp.concatenate([request, paired_ids], axis=0)
    qheads = qnorm.reshape(rows, head_count, HD)
    kheads = all_keys.reshape(rows + SHARE, head_count, HD)
    scores = jnp.einsum(
        "qhd,khd->hqk", qheads, kheads, preferred_element_type=jnp.float32
    ) / math.sqrt(HD)
    same = request[:, None] == all_ids[None, :]
    scores = jnp.where(same[None], scores, -jnp.inf)
    top = jnp.max(scores, axis=-1, keepdims=True)
    expo = jnp.exp(scores - top)
    probs = (expo / jnp.sum(expo, axis=-1, keepdims=True)).astype(jnp.bfloat16)
    value = jnp.dot(normed, w_v, preferred_element_type=jnp.float32).astype(jnp.bfloat16)
    value_window = lax.dynamic_slice_in_dim(value, seam, SHARE, 0)
    all_values = jnp.concatenate([value, swapped(value_window, "group", 0)], axis=0)
    vheads = all_values.reshape(rows + SHARE, head_count, HD)
    attended = jnp.einsum("hqk,khd->qhd", probs, vheads, preferred_element_type=jnp.float32)
    attended = attended.astype(jnp.bfloat16).reshape(rows, local_width)
    branch = jnp.zeros((rows, feat_local), jnp.float32)
    for step in range(tp_count):
        onward = from_next(attended, "tp") if step < tp_count - 1 else None
        part = lax.dot_general(
            attended, w_o[step], (((1,), (1,)), ((), ())), preferred_element_type=jnp.float32
        )
        branch = branch + part.astype(jnp.bfloat16).astype(jnp.float32)
        attended = onward
    mixed = (tokens.astype(jnp.float32) + layer_scale * branch).astype(jnp.bfloat16)
    capacity = max(2, 2 * rows // group_count)
    target = owner[:, 0]
    onehot = (target[:, None] == jnp.arange(group_count, dtype=jnp.int32)[None, :]).astype(
        jnp.int32
    )
    slot = jnp.sum((jnp.cumsum(onehot, axis=0) - onehot) * onehot, axis=-1)
    place = target * capacity + slot
    select = (
        jnp.arange(group_count * capacity, dtype=jnp.int32)[:, None] == place[None, :]
    ).astype(jnp.bfloat16)
    outbox = jnp.dot(select, mixed, preferred_element_type=jnp.float32).astype(jnp.bfloat16)
    outbox = outbox.reshape(group_count, capacity, feat_local)
    inbox = lax.all_to_all(outbox, "group", split_axis=0, concat_axis=0, tiled=True)
    return inbox[None]


def solution(mesh):
    in_specs = (
        P("group", "tp"),
        P("tp"),
        P("group", None, "tp"),
        P(None, "tp"),
        P("tp", "group"),
        P("tp"),
        P("group"),
        P("group", None),
    )
    out_specs = P("group", None, None, "tp")
    return jax.shard_map(shards, mesh=mesh, in_specs=in_specs, out_specs=out_specs, check_vma=False)
```

profile of v0, /device:TPU:1, one launch (start us, length us, event | category | flops | bytes accessed | tf_op | source)
XLA Modules:
  0.0 388.7 jit_solution(6893190634772849694)
XLA Ops:
  6.5 0.0 all-gather.13.cloned.1.call-start
  6.5 2.3 fusion.44
  8.8 0.0 all-gather.13.cloned.1.call-update
  8.9 0.0 all-gather.11.cloned.1.call-start
  8.9 0.7 all-gather.11.cloned.1.call-update
  9.6 0.0 all-gather.7.cloned.1.call-start
  9.7 2.1 collective-permute-start
  11.8 0.2 broadcast_in_dim.16
  12.0 0.0 copy-start.3
  12.0 0.0 copy-start.4
  12.0 0.0 copy-start.5
  12.0 1.6 constant_dynamic-update-slice_fusion.1
  13.6 34.0 %collective-permute-done = bf16[512,1600]{0,1:T(8,128)(2,1)} collective-permute-done((bf16[512,1600]{0,1:T(8,128)(2,1)}, bf16[512,1600]{0,1:T(8,128)(2,1)}, u32[]{:S(2)}, u32[]{:S(2)}) %collective-permute-start) | collective-permute-done | bytes 1638432 | tf_op jit(solution)/shard_map/ppermute | solution.py:19
  47.6 1.6 constant_dynamic-update-slice_fusion
  49.2 0.0 all-gather.7.cloned.1.call-update
  49.2 0.0 all-gather.9.cloned.1.call-start
  49.3 4.9 %collective-permute-start.5 = (bf16[200,1024]{1,0:T(8,128)(2,1)}, bf16[200,1024]{1,0:T(8,128)(2,1)}, u32[]{:S(2)}, u32[]{:S(2)}) collective-permute-start(bf16[200,1024]{1,0:T(8,128)(2,1)} %bitcast.70), channel_id=1, source_target_pairs={{0,0},{1,16},{2,2},{3,18},{4,4},{5,20},{6,6},{7,22},{8,8},{9,24},{... | collective-permute-start | bytes 1228808 | tf_op jit(solution)/shard_map/ppermute | solution.py:48
  54.2 0.0 collective-permute-done.5
  54.2 0.0 all-gather.9.cloned.1.call-update
  54.2 0.0 copy-done.3
  54.2 35.8 %collective-permute-start.1 = (bf16[1,1600]{1,0:T(2,128)(2,1)S(1)}, bf16[1,1600]{1,0:T(2,128)(2,1)S(1)}, u32[]{:S(2)}, u32[]{:S(2)}) collective-permute-start(bf16[1,1600]{1,0:T(2,128)(2,1)S(1)} %reshape.93), channel_id=1, source_target_pairs={{1,0},{0,1},{3,2},{2,3},{5,4},{4,5},{7,6},{6,7},{9,8},{8,9},{11,10... | collective-permute-start | bytes 9608 | tf_op jit(solution)/shard_map/ppermute | solution.py:19
  90.0 0.0 copy-done.4
  90.0 0.1 dynamic_slice.10
  90.1 0.9 collective-permute-start.3
  91.0 0.0 copy-done.5
  91.1 0.3 dynamic_update_slice.16
  91.4 0.5 collective-permute-done.3
  91.9 0.0 collective-permute-done.1
  91.9 0.3 dynamic_update_slice.17
  92.2 0.8 fusion.2
  93.0 0.0 all-gather.13.cloned.1.call-done
  93.0 8.0 %multiply_reduce_fusion = (f32[512]{0:T(512)S(1)}, f32[512,1024]{1,0:T(8,128)}) fusion(bf16[3200,1,1024]{2,0,1:T(8,128)(2,1)} %all-gather.13.cloned.1.call-done, bf16[512,3200]{0,1:T(8,128)(2,1)S(1)} %constant_dynamic-update-slice_fusion, f32[3200]{0:T(1024)S(1)} %mul.106, f32[512]{0:T(512)S(1)} %add_rsqrt_fusion.2), kind=kOutput, calls=%fused_computation.27 | convolution fusion | flops 3363044864 | bytes 11944448 | tf_op jit(solution)/shard_map/dot_general | solution.py:54
  101.0 53.1 %all-gather.11.cloned.1.call-done = bf16[3200,1,1024]{2,0,1:T(8,128)(2,1)} async-done(((bf16[200,1,1024]{2,0,1:T(8,128)(2,1)}), bf16[3200,1,1024]{2,0,1:T(8,128)(2,1)}) %all-gather.11.cloned.1.call-update) | async-done | bytes 6553616 | tf_op jit(solution)/shard_map/all_gather | solution.py:29
  154.1 8.0 %multiply_reduce_fusion.1 = (f32[512]{0:T(512)S(1)}, f32[512,1024]{1,0:T(8,128)}) fusion(bf16[3200,1,1024]{2,0,1:T(8,128)(2,1)} %all-gather.11.cloned.1.call-done, bf16[512,3200]{0,1:T(8,128)(2,1)S(1)} %constant_dynamic-update-slice_fusion, f32[3200]{0:T(1024)S(1)} %mul.106, f32[512]{0:T(512)S(1)} %add_rsqrt_fusion.2), kind=kOutput, calls=%fused_computation.29 | convolution fusion | flops 3363044864 | bytes 11944448 | tf_op jit(solution)/shard_map/dot_general | solution.py:55
  162.1 4.3 %all-reduce = (f32[512]{0:T(512)S(1)}, f32[512]{0:T(512)S(1)}) all-reduce(f32[512]{0:T(512)S(1)} %get-tuple-element.18, f32[512]{0:T(512)S(1)} %get-tuple-element.20), channel_id=1, replica_groups=mesh['group'=16,'tp'=2] {'tp'}, use_global_device_ids=true, to_apply=%region_7.8 | all-reduce | flops 1024 | bytes 8192 | tf_op jit(solution)/shard_map/psum | solution.py:56
  166.4 2.0 multiply_convert_fusion
  168.5 1.1 collective-permute-start.4
  169.5 1.0 broadcast_compare_fusion
  170.5 0.2 collective-permute-done.4
  170.7 0.0 copy-done
  170.7 5.6 %fusion.26 = f32[8,512,640]{2,1,0:T(8,128)} fusion(bf16[128,1024]{1,0:T(8,128)(2,1)S(1)} %collective-permute-done.4, bf16[512,1024]{1,0:T(8,128)(2,1)S(1)} %multiply_convert_fusion, f32[512,1024]{1,0:T(8,128)S(1)} %copy-done, f32[1024]{0:T(1024)S(1)} %bitcast.66, f32[512]{0:T(512)S(1)} %add_rsqrt_fusion.1), kind=kOutput, calls=%fused_computation.33 | convolution fusion | flops 675282944 | bytes 13899776 | tf_op jit(solution)/shard_map/qhd,khd->hqk/dot_general | solution.py:75
  176.3 42.1 %all-gather.7.cloned.1.call-done = bf16[3200,1024]{1,0:T(8,128)(2,1)} async-done(((bf16[200,1024]{1,0:T(8,128)(2,1)}), bf16[3200,1024]{1,0:T(8,128)(2,1)}) %all-gather.7.cloned.1.call-update) | async-done | bytes 6553616 | tf_op jit(solution)/shard_map/all_gather | solution.py:40
  218.3 6.7 %convolution_convert_fusion.1 = bf16[512,1024]{1,0:T(8,128)(2,1)S(1)} fusion(bf16[3200,1024]{1,0:T(8,128)(2,1)} %all-gather.7.cloned.1.call-done, bf16[512,3200]{0,1:T(8,128)(2,1)S(1)} %constant_dynamic-update-slice_fusion, f32[3200]{0:T(1024)S(1)} %mul.106, f32[512]{0:T(512)S(1)} %add_rsqrt_fusion.2), kind=kOutput, calls=%fused_computation.32 | convolution fusion | flops 3362521088 | bytes 10893824 | tf_op jit(solution)/shard_map/dot_general | solution.py:83
  225.1 0.3 collective-permute-start.2
  225.4 0.0 copy-done.1
  225.4 15.4 %fusion.46 = (f32[8,512]{1,0:T(8,128)S(1)}, f32[8,512,640]{2,1,0:T(8,128)}) fusion(f32[8,512,640]{2,1,0:T(8,128)} %fusion.26, pred[512,640]{1,0:T(8,128)(4,1)S(1)} %copy-done.1), kind=kOutput, calls=%fused_computation.66 | output fusion | flops 15729279 | bytes 21315584 | tf_op jit(solution)/shard_map/sub | solution.py:81
  240.8 0.0 collective-permute-done.2
  240.8 0.1 pad_maximum_fusion
  240.9 1.0 copy.18
  241.9 0.0 copy-start.2
  241.9 6.0 %fusion.25 = bf16[8,128,512]{2,1,0:T(8,128)(2,1)S(1)} fusion(bf16[640,8,128]{0,2,1:T(8,128)(2,1)S(1)} %bitcast.62, f32[8,512,640]{2,1,0:T(8,128)} %get-tuple-element.23, f32[8,512]{1,0:T(8,128)S(1)} %get-tuple-element.22), kind=kOutput, calls=%fused_computation.31 | convolution fusion | flops 676855808 | bytes 12861440 | tf_op jit(solution)/shard_map/hqk,khd->qhd/dot_general | solution.py:87
  247.9 1.3 collective-permute-start.6
  249.2 0.0 copy-done.2
  249.2 1.2 reduce-window.6
  250.3 0.2 slice_reduce_fusion
  250.6 0.1 fusion.37
  250.7 0.0 copy-start.6
  250.7 31.7 %all-gather.9.cloned.1.call-done = bf16[3200,1024]{1,0:T(8,128)(2,1)} async-done(((bf16[200,1024]{1,0:T(8,128)(2,1)}), bf16[3200,1024]{1,0:T(8,128)(2,1)}) %all-gather.9.cloned.1.call-update) | async-done | bytes 6553616 | tf_op jit(solution)/shard_map/all_gather | solution.py:49
  282.4 5.0 %fusion.17 = bf16[512,1600]{0,1:T(8,128)(2,1)} fusion(bf16[512,1024]{0,1:T(8,128)(2,1)S(1)} %bitcast.69, bf16[3200,1024]{1,0:T(8,128)(2,1)} %all-gather.9.cloned.1.call-done), kind=kOutput, calls=%fused_computation.24 | convolution fusion | flops 1678540800 | bytes 5963776 | tf_op jit(solution)/shard_map/dot_general | solution.py:92
  287.4 0.0 collective-permute-done.6
  287.4 8.5 %convolution_convert_fusion = bf16[1024,1600]{0,1:T(8,128)(2,1)} fusion(s32[512]{0:T(512)S(1)} %multiply_add_fusion, bf16[512,1600]{0,1:T(8,128)(2,1)} %fusion.17, bf16[512,1600]{0,1:T(8,128)(2,1)} %param.8, bf16[512,1024]{0,1:T(8,128)(2,1)S(1)} %collective-permute-done.6, bf16[3200,1024]{1,0:T(8,128)(2,1)} %all-gather.9.cloned.1.call-done, ...), kind=kOutput, calls=%fused_computation.18 | convolution fusion | flops 3364159488 | bytes 10887424 | tf_op jit(solution)/shard_map/dot_general | solution.py:108
  295.9 4.3 %copy.17 = bf16[1024,1600]{1,0:T(8,128)(2,1)S(1)} copy(bf16[1024,1600]{0,1:T(8,128)(2,1)} %convolution_convert_fusion) | data formatting | bytes 6553600 | tf_op jit(solution)/shard_map/convert_element_type | solution.py:108
  300.3 80.1 %all_to_all.5 = bf16[16,64,1600]{2,1,0:T(8,128)(2,1)S(1)} all-to-all(bf16[16,64,1600]{2,1,0:T(8,128)(2,1)S(1)} %bitcast.60), channel_id=1, replica_groups=mesh['group'=16,'tp'=2] {'group'}, dimensions={0} | all-to-all | bytes 6553600 | tf_op jit(solution)/shard_map/all_to_all | solution.py:110
  380.4 1.8 copy.36
  (18 shorter events, 0.2 us)
Async XLA Ops:
  6.5 86.5 %all-gather.13.cloned.1.call-start = ((), (), s32[]{:S(2)}) async-start(), calls=%async_computation.4 | async-start | bytes 6963200 | tf_op jit(solution)/shard_map/all_gather | solution.py:29
  8.9 145.2 %all-gather.11.cloned.1.call-start = ((), (), s32[]{:S(2)}) async-start(), calls=%async_computation.3 | async-start | bytes 6963200 | tf_op jit(solution)/shard_map/all_gather | solution.py:29
  9.6 208.7 %all-gather.7.cloned.1.call-start = ((), (), s32[]{:S(2)}) async-start(), calls=%async_computation.1 | async-start | bytes 6963200 | tf_op jit(solution)/shard_map/all_gather | solution.py:40
  9.7 38.0 %collective-permute-start = (bf16[512,1600]{0,1:T(8,128)(2,1)}, bf16[512,1600]{0,1:T(8,128)(2,1)}, u32[]{:S(2)}, u32[]{:S(2)}) collective-permute-start(bf16[512,1600]{0,1:T(8,128)(2,1)} %param.8), channel_id=1, source_target_pairs={{1,0},{0,1},{3,2},{2,3},{5,4},{4,5},{7,6},{6,7},{9,8},{8,9},{11,10... | collective-permute-start | bytes 4915208 | tf_op jit(solution)/shard_map/ppermute | solution.py:19
  12.0 42.2 %copy-start.3 = (bf16[1600]{0:T(1024)(128)(2,1)S(1)}, bf16[1600]{0:T(1024)(128)(2,1)}, u32[]{:S(2)}) copy-start(bf16[1600]{0:T(1024)(128)(2,1)} %param.9) | copy-start | bytes 9604
  12.0 78.0 %copy-start.4 = (s32[512]{0:T(512)S(1)}, s32[512]{0:T(512)}, u32[]{:S(2)}) copy-start(s32[512]{0:T(512)} %param.14) | copy-start | bytes 6148
  12.0 79.0 %copy-start.5 = (f32[2,1024]{1,0:T(2,128)S(1)}, f32[2,1024]{1,0:T(2,128)}, u32[]{:S(2)}) copy-start(f32[2,1024]{1,0:T(2,128)} %param.11) | copy-start | bytes 24580
  49.2 233.2 %all-gather.9.cloned.1.call-start = ((), (), s32[]{:S(2)}) async-start(), calls=%async_computation.2 | async-start | bytes 6963200 | tf_op jit(solution)/shard_map/all_gather | solution.py:49
  49.3 4.9 %collective-permute-start.5 = (bf16[200,1024]{1,0:T(8,128)(2,1)}, bf16[200,1024]{1,0:T(8,128)(2,1)}, u32[]{:S(2)}, u32[]{:S(2)}) collective-permute-start(bf16[200,1024]{1,0:T(8,128)(2,1)} %bitcast.70), channel_id=1, source_target_pairs={{0,0},{1,16},{2,2},{3,18},{4,4},{5,20},{6,6},{7,22},{8,8},{9,24},{... | collective-permute-start | bytes 1228808 | tf_op jit(solution)/shard_map/ppermute | solution.py:48
  54.2 37.6 %collective-permute-start.1 = (bf16[1,1600]{1,0:T(2,128)(2,1)S(1)}, bf16[1,1600]{1,0:T(2,128)(2,1)S(1)}, u32[]{:S(2)}, u32[]{:S(2)}) collective-permute-start(bf16[1,1600]{1,0:T(2,128)(2,1)S(1)} %reshape.93), channel_id=1, source_target_pairs={{1,0},{0,1},{3,2},{2,3},{5,4},{4,5},{7,6},{6,7},{9,8},{8,9},{11,10... | collective-permute-start | bytes 9608 | tf_op jit(solution)/shard_map/ppermute | solution.py:19
  90.1 1.8 collective-permute-start.3
  166.4 4.3 %copy-start = (f32[512,1024]{1,0:T(8,128)S(1)}, f32[512,1024]{1,0:T(8,128)}, u32[]{:S(2)}) copy-start(f32[512,1024]{1,0:T(8,128)} %get-tuple-element.21) | copy-start | bytes 6291460
  168.5 2.2 collective-permute-start.4
  218.3 7.1 %copy-start.1 = (pred[512,640]{1,0:T(8,128)(4,1)S(1)}, pred[512,640]{1,0:T(8,128)(4,1)}, u32[]{:S(2)}) copy-start(pred[512,640]{1,0:T(8,128)(4,1)} %broadcast_compare_fusion) | copy-start | bytes 983044
  225.1 15.7 %collective-permute-start.2 = (bf16[128,1024]{1,0:T(8,128)(2,1)S(1)}, bf16[128,1024]{1,0:T(8,128)(2,1)S(1)}, u32[]{:S(2)}, u32[]{:S(2)}) collective-permute-start(bf16[128,1024]{1,0:T(8,128)(2,1)S(1)} %constant_dynamic-slice_fusion.1), channel_id=1, source_target_pairs={{0,2},{2,0},{4,6},{6,4},{8,10},{10,8},{12,14},{14,12},{16,18},{18,... | collective-permute-start | bytes 786440 | tf_op jit(solution)/shard_map/ppermute | solution.py:14
  241.9 7.3 %copy-start.2 = (s32[512,1]{0,1:T(1,128)S(1)}, s32[512,1]{0,1:T(1,128)}, u32[]{:S(2)}) copy-start(s32[512,1]{0,1:T(1,128)} %param.15) | copy-start | bytes 6148
  247.9 39.5 %collective-permute-start.6 = (bf16[512,1024]{0,1:T(8,128)(2,1)S(1)}, bf16[512,1024]{0,1:T(8,128)(2,1)S(1)}, u32[]{:S(2)}, u32[]{:S(2)}) collective-permute-start(bf16[512,1024]{0,1:T(8,128)(2,1)S(1)} %bitcast.68), channel_id=1, source_target_pairs={{1,0},{0,1},{3,2},{2,3},{5,4},{4,5},{7,6},{6,7},{9,8},{8,9},{11,10... | collective-permute-start | bytes 3145736 | tf_op jit(solution)/shard_map/ppermute | solution.py:19
  250.7 36.7 %copy-start.6 = (f32[1600]{0:T(1024)S(1)}, f32[1600]{0:T(1024)}, u32[]{:S(2)}) copy-start(f32[1600]{0:T(1024)} %param.13) | copy-start | bytes 19204
Sparse Core Ops, SparseCore 0:
  9.6 65.8 all-gather.12
  77.9 76.1 all-gather.10
  156.3 61.9 all-gather.6
  220.5 61.8 all-gather.8
where the time goes:
time: 389 us
  waiting for transfers between devices  162 us (42%)
  blocking collectives  84.5 us (22%)
  matrix products  47.7 us (12%)
  starting transfers between devices  46.6 us (12%)
  other arithmetic  20.6 us (5%)
  local copies, waits for them, and re-layouts  13.7 us (4%)
  between operations  13.3 us (3%)
    all_to_all x1, blocking collectives, shards(): lax.all_to_all(outbox, 'group', split_axis=0, concat_axis=0, tiled=True)  80.1 us
    all_gather x2, waiting for transfers between devices, shards(): lax.all_gather(w_qkv[:, i, :], 'group', axis=0, tiled=True)  53.1 us
    all_gather x1, waiting for transfers between devices, shards(): w_v = lax.all_gather(late_v, 'group', axis=0, tiled=True)  42.1 us
    ppermute x3, starting transfers between devices, from_next(): lax.ppermute(value, axis, [((i + 1) % count, i) for i in range(count)])  39.2 us
    ppermute x3, waiting for transfers between devices, from_next(): lax.ppermute(value, axis, [((i + 1) % count, i) for i in range(count)])  34 us
    all_gather x1, waiting for transfers between devices, shards(): w_o = lax.all_gather(w_piece, 'group', axis=0, tiled=True)  31.7 us
    sub x1, other arithmetic, shards(): expo = jnp.exp(scores - top)  15.4 us
    dot_general x1, matrix products, shards(): jnp.dot(select, mixed, preferred_element_type=jnp.float32)  8.52 us
  transfers between devices with their start and end apart: 11, of which 6 were waited for; matrix products, arithmetic and copies ran while one was open for 17% of the time, Pallas kernels for 0%

commit v1 on v0

--- a/solution.py
+++ b/solution.py
@@ -37,7 +37,6 @@
         if step < tp_count - 1:
             piece, gain = (from_next(piece, "tp"), from_next(gain, "tp"))
     whole, late_v, late_out = lax.optimization_barrier((whole, w_qkv[:, 2, :], w_out))
-    w_v = lax.all_gather(late_v, "group", axis=0, tiled=True)
     per = group_count // tp_count
     pairs = []
     for g in range(group_count):
@@ -46,7 +45,11 @@
             to_g = (b - t) % tp_count * per + j
             pairs.append((g * tp_count + b, to_g * tp_count + t))
     w_piece = lax.ppermute(late_out.T, ("group", "tp"), pairs)
-    w_o = lax.all_gather(w_piece, "group", axis=0, tiled=True)
+    w_v, w_o = jnp.split(
+        lax.all_gather(jnp.concatenate([late_v, w_piece], axis=1), "group", axis=0, tiled=True),
+        [late_v.shape[1]],
+        axis=1,
+    )
     w_o = w_o.reshape(tp_count, feat_local, local_width)
     xwide = whole.astype(jnp.float32)
     stat = jnp.mean(xwide * xwide, axis=-1, keepdims=True)

time: 389 us -> 415 us (1.067)
  waiting for transfers between devices: 162 us -> 187 us
    ppermute x3, waiting for transfers between devices: 34 us -> 50.7 us  [from_next(): lax.ppermute(value, axis, [((i + 1) % count, i) for i in range(count)])]
    all_gather x2 -> x1, waiting for transfers between devices: 73.8 us -> 82.8 us  [shards(): lax.all_gather(jnp.concatenate([late_v, w_piece], axis=1), 'group', axis=...]
    ppermute x1, starting transfers between devices: 4.91 us -> 0.69 us  [shards(): w_piece = lax.ppermute(late_out.T, ('group', 'tp'), pairs)]
    ppermute x3, starting transfers between devices: 39.2 us -> 43.4 us  [from_next(): lax.ppermute(value, axis, [((i + 1) % count, i) for i in range(count)])]
  transfers between devices with their start and end apart: 11 -> 10, of which waited for: 6 -> 6; matrix products, arithmetic and copies ran while one was open for 17% -> 13% of each run, Pallas kernels for 0% -> 0%
where the time goes in v1:
time: 415 us; the launch traced here: 414 us
  waiting for transfers between devices  187 us (45%)
  blocking collectives  84.8 us (20%)
  matrix products  47.6 us (11%)
  starting transfers between devices  46.4 us (11%)
  other arithmetic  21.2 us (5%)
  local copies, waits for them, and re-layouts  13.8 us (3%)
  between operations  13.3 us (3%)
    all_gather x1, waiting for transfers between devices, shards(): lax.all_gather(jnp.concatenate([late_v, w_piece], axis=1), 'group', axis=...  82.8 us
    all_to_all x1, blocking collectives, shards(): lax.all_to_all(outbox, 'group', split_axis=0, concat_axis=0, tiled=True)  80.4 us
    all_gather x2, waiting for transfers between devices, shards(): lax.all_gather(w_qkv[:, i, :], 'group', axis=0, tiled=True)  52.3 us
    ppermute x3, waiting for transfers between devices, from_next(): lax.ppermute(value, axis, [((i + 1) % count, i) for i in range(count)])  50.7 us
    ppermute x3, starting transfers between devices, from_next(): lax.ppermute(value, axis, [((i + 1) % count, i) for i in range(count)])  43.4 us
    sub x1, other arithmetic, shards(): expo = jnp.exp(scores - top)  15 us
    dot_general x1, matrix products, shards(): jnp.dot(select, mixed, preferred_element_type=jnp.float32)  8.52 us
  transfers between devices with their start and end apart: 10, of which 6 were waited for; matrix products, arithmetic and copies ran while one was open for 13% of the time, Pallas kernels for 0%

profile of v1, /device:TPU:1, one launch (start us, length us, event | category | flops | bytes accessed | tf_op | source)
XLA Modules:
  0.0 414.4 jit_solution(11370718658978917050)
XLA Ops:
  6.5 0.0 all-gather.8.cloned.1.call-start
  6.5 2.3 fusion.49
  8.8 0.0 all-gather.8.cloned.1.call-update
  8.9 0.0 all-gather.10.cloned.1.call-start
  8.9 0.7 all-gather.10.cloned.1.call-update
  9.6 0.0 all-gather.6.cloned.1.call-start
  9.7 2.1 collective-permute-start
  11.8 0.2 broadcast_in_dim.16
  12.0 0.0 copy-start.7
  12.0 0.0 copy-start.1
  12.0 1.7 constant_dynamic-update-slice_fusion.1
  13.7 0.0 copy-start.4
  13.7 0.0 copy-start.5
  13.7 0.0 copy-start.6
  13.7 33.9 %collective-permute-done = bf16[512,1600]{0,1:T(8,128)(2,1)} collective-permute-done((bf16[512,1600]{0,1:T(8,128)(2,1)}, bf16[512,1600]{0,1:T(8,128)(2,1)}, u32[]{:S(2)}, u32[]{:S(2)}) %collective-permute-start) | collective-permute-done | bytes 1638432 | tf_op jit(solution)/shard_map/ppermute | solution.py:19
  47.6 1.6 constant_dynamic-update-slice_fusion
  49.2 0.0 copy-done.7
  49.2 0.7 collective-permute-start.2
  49.9 0.0 collective-permute-done.2
  49.9 0.0 copy-done.1
  49.9 1.0 pad_maximum_fusion.1
  50.9 0.0 all-gather.6.cloned.1.call-update
  50.9 0.0 copy-done.4
  50.9 40.0 %collective-permute-start.1 = (bf16[1,1600]{1,0:T(2,128)(2,1)S(1)}, bf16[1,1600]{1,0:T(2,128)(2,1)S(1)}, u32[]{:S(2)}, u32[]{:S(2)}) collective-permute-start(bf16[1,1600]{1,0:T(2,128)(2,1)S(1)} %reshape.93), channel_id=1, source_target_pairs={{1,0},{0,1},{3,2},{2,3},{5,4},{4,5},{7,6},{6,7},{9,8},{8,9},{11,10... | collective-permute-start | bytes 9608 | tf_op jit(solution)/shard_map/ppermute | solution.py:19
  90.9 0.0 copy-done.5
  90.9 0.1 dynamic_slice.10
  91.0 0.9 collective-permute-start.4
  91.9 0.3 dynamic_update_slice.16
  92.2 0.5 collective-permute-done.4
  92.7 0.0 collective-permute-done.1
  92.8 0.3 dynamic_update_slice.17
  93.1 0.8 fusion.2
  93.8 0.0 all-gather.8.cloned.1.call-done
  93.8 8.0 %multiply_reduce_fusion.1 = (f32[512]{0:T(512)S(1)}, f32[512,1024]{1,0:T(8,128)}) fusion(bf16[3200,1,1024]{2,0,1:T(8,128)(2,1)} %all-gather.8.cloned.1.call-done, bf16[512,3200]{0,1:T(8,128)(2,1)S(1)} %constant_dynamic-update-slice_fusion, f32[3200]{0:T(1024)S(1)} %mul.106, f32[512]{0:T(512)S(1)} %add_rsqrt_fusion.2), kind=kOutput, calls=%fused_computation.31 | convolution fusion | flops 3363044864 | bytes 11944448 | tf_op jit(solution)/shard_map/dot_general | solution.py:58
  101.8 52.3 %all-gather.10.cloned.1.call-done = bf16[3200,1,1024]{2,0,1:T(8,128)(2,1)} async-done(((bf16[200,1,1024]{2,0,1:T(8,128)(2,1)}), bf16[3200,1,1024]{2,0,1:T(8,128)(2,1)}) %all-gather.10.cloned.1.call-update) | async-done | bytes 6553616 | tf_op jit(solution)/shard_map/all_gather | solution.py:29
  154.1 8.0 %multiply_reduce_fusion = (f32[512]{0:T(512)S(1)}, f32[512,1024]{1,0:T(8,128)}) fusion(bf16[3200,1,1024]{2,0,1:T(8,128)(2,1)} %all-gather.10.cloned.1.call-done, bf16[512,3200]{0,1:T(8,128)(2,1)S(1)} %constant_dynamic-update-slice_fusion, f32[3200]{0:T(1024)S(1)} %mul.106, f32[512]{0:T(512)S(1)} %add_rsqrt_fusion.2), kind=kOutput, calls=%fused_computation.29 | convolution fusion | flops 3363044864 | bytes 11944448 | tf_op jit(solution)/shard_map/dot_general | solution.py:57
  162.1 4.3 %all-reduce = (f32[512]{0:T(512)S(1)}, f32[512]{0:T(512)S(1)}) all-reduce(f32[512]{0:T(512)S(1)} %get-tuple-element.18, f32[512]{0:T(512)S(1)} %get-tuple-element.20), channel_id=1, replica_groups=mesh['group'=16,'tp'=2] {'tp'}, use_global_device_ids=true, to_apply=%region_7.8 | all-reduce | flops 1024 | bytes 8192 | tf_op jit(solution)/shard_map/psum | solution.py:59
  166.5 2.0 multiply_convert_fusion
  168.5 1.1 collective-permute-start.5
  169.6 1.0 broadcast_compare_fusion
  170.5 0.2 collective-permute-done.5
  170.7 5.5 %fusion.31 = f32[8,512,640]{2,1,0:T(8,128)} fusion(bf16[128,1024]{1,0:T(8,128)(2,1)S(1)} %collective-permute-done.5, bf16[512,1024]{1,0:T(8,128)(2,1)S(1)} %multiply_convert_fusion, f32[512,1024]{1,0:T(8,128)S(1)} %copy-done, f32[1024]{0:T(1024)S(1)} %bitcast.65, f32[512]{0:T(512)S(1)} %add_rsqrt_fusion.1), kind=kOutput, calls=%fused_computation.35 | convolution fusion | flops 675282944 | bytes 13899776 | tf_op jit(solution)/shard_map/qhd,khd->hqk/dot_general | solution.py:78
  176.2 82.8 %all-gather.6.cloned.1.call-done = bf16[3200,2048]{1,0:T(8,128)(2,1)} async-done(((bf16[200,2048]{1,0:T(8,128)(2,1)}), bf16[3200,2048]{1,0:T(8,128)(2,1)}) %all-gather.6.cloned.1.call-update) | async-done | bytes 13107216 | tf_op jit(solution)/shard_map/all_gather | solution.py:49
  259.0 6.7 %fusion.28 = bf16[512,1024]{1,0:T(8,128)(2,1)S(1)} fusion(bf16[3200,2048]{1,0:T(8,128)(2,1)} %all-gather.6.cloned.1.call-done, bf16[512,3200]{0,1:T(8,128)(2,1)S(1)} %constant_dynamic-update-slice_fusion, f32[3200]{0:T(1024)S(1)} %mul.106, f32[512]{0:T(512)S(1)} %add_rsqrt_fusion.2), kind=kOutput, calls=%fused_computation.34 | convolution fusion | flops 3362521088 | bytes 10893824 | tf_op jit(solution)/shard_map/dot_general | solution.py:86
  265.8 0.3 collective-permute-start.3
  266.1 0.0 copy-done.2
  266.1 15.0 %fusion.51 = (f32[8,512]{1,0:T(8,128)S(1)}, f32[8,512,640]{2,1,0:T(8,128)}) fusion(f32[8,512,640]{2,1,0:T(8,128)} %fusion.31, pred[512,640]{1,0:T(8,128)(4,1)S(1)} %copy-done.2), kind=kOutput, calls=%fused_computation.69 | output fusion | flops 15729279 | bytes 21315584 | tf_op jit(solution)/shard_map/sub | solution.py:84
  281.1 0.0 collective-permute-done.3
  281.1 0.1 pad_maximum_fusion
  281.2 1.0 copy.18
  282.2 0.0 copy-start.3
  282.2 6.0 %fusion.27 = bf16[8,128,512]{2,1,0:T(8,128)(2,1)S(1)} fusion(bf16[640,8,128]{0,2,1:T(8,128)(2,1)S(1)} %bitcast.61, f32[8,512,640]{2,1,0:T(8,128)} %get-tuple-element.23, f32[8,512]{1,0:T(8,128)S(1)} %get-tuple-element.22), kind=kOutput, calls=%fused_computation.33 | convolution fusion | flops 676855808 | bytes 12861440 | tf_op jit(solution)/shard_map/hqk,khd->qhd/dot_general | solution.py:90
  288.2 1.3 collective-permute-start.6
  289.4 0.0 copy-done.3
  289.5 1.2 reduce-window.6
  290.6 0.2 slice_reduce_fusion
  290.9 0.1 fusion.42
  291.0 0.0 copy-start.8
  291.0 5.0 %fusion.19 = bf16[512,1600]{0,1:T(8,128)(2,1)} fusion(bf16[512,1024]{0,1:T(8,128)(2,1)S(1)} %bitcast.68, bf16[3200,2048]{1,0:T(8,128)(2,1)} %all-gather.6.cloned.1.call-done), kind=kOutput, calls=%fused_computation.26 | convolution fusion | flops 1678540800 | bytes 5963776 | tf_op jit(solution)/shard_map/dot_general | solution.py:95
  296.0 16.8 %collective-permute-done.6 = bf16[512,1024]{0,1:T(8,128)(2,1)S(1)} collective-permute-done((bf16[512,1024]{0,1:T(8,128)(2,1)S(1)}, bf16[512,1024]{0,1:T(8,128)(2,1)S(1)}, u32[]{:S(2)}, u32[]{:S(2)}) %collective-permute-start.6) | collective-permute-done | bytes 1048608 | tf_op jit(solution)/shard_map/ppermute | solution.py:19
  312.8 8.5 %convolution_convert_fusion = bf16[1024,1600]{0,1:T(8,128)(2,1)} fusion(s32[512]{0:T(512)S(1)} %multiply_add_fusion, bf16[512,1600]{0,1:T(8,128)(2,1)} %fusion.19, bf16[512,1600]{0,1:T(8,128)(2,1)} %param.8, bf16[512,1024]{0,1:T(8,128)(2,1)S(1)} %collective-permute-done.6, bf16[3200,2048]{1,0:T(8,128)(2,1)} %all-gather.6.cloned.1.call-done, ...), kind=kOutput, calls=%fused_computation.20 | convolution fusion | flops 3364159488 | bytes 10887424 | tf_op jit(solution)/shard_map/dot_general | solution.py:111
  321.3 4.3 %copy.17 = bf16[1024,1600]{1,0:T(8,128)(2,1)S(1)} copy(bf16[1024,1600]{0,1:T(8,128)(2,1)} %convolution_convert_fusion) | data formatting | bytes 6553600 | tf_op jit(solution)/shard_map/convert_element_type | solution.py:111
  325.6 80.4 %all_to_all.5 = bf16[16,64,1600]{2,1,0:T(8,128)(2,1)S(1)} all-to-all(bf16[16,64,1600]{2,1,0:T(8,128)(2,1)S(1)} %bitcast.59), channel_id=1, replica_groups=mesh['group'=16,'tp'=2] {'group'}, dimensions={0} | all-to-all | bytes 6553600 | tf_op jit(solution)/shard_map/all_to_all | solution.py:113
  406.1 1.8 copy.36
  (20 shorter events, 0.2 us)
Async XLA Ops:
  6.5 87.3 %all-gather.8.cloned.1.call-start = ((), (), s32[]{:S(2)}) async-start(), calls=%async_computation.2 | async-start | bytes 6963200 | tf_op jit(solution)/shard_map/all_gather | solution.py:29
  8.9 145.3 %all-gather.10.cloned.1.call-start = ((), (), s32[]{:S(2)}) async-start(), calls=%async_computation.3 | async-start | bytes 6963200 | tf_op jit(solution)/shard_map/all_gather | solution.py:29
  9.6 249.4 %all-gather.6.cloned.1.call-start = ((), (), s32[]{:S(2)}) async-start(), calls=%async_computation.1 | async-start | bytes 13926400 | tf_op jit(solution)/shard_map/all_gather | solution.py:49
  9.7 38.0 %collective-permute-start = (bf16[512,1600]{0,1:T(8,128)(2,1)}, bf16[512,1600]{0,1:T(8,128)(2,1)}, u32[]{:S(2)}, u32[]{:S(2)}) collective-permute-start(bf16[512,1600]{0,1:T(8,128)(2,1)} %param.8), channel_id=1, source_target_pairs={{1,0},{0,1},{3,2},{2,3},{5,4},{4,5},{7,6},{6,7},{9,8},{8,9},{11,10... | collective-permute-start | bytes 4915208 | tf_op jit(solution)/shard_map/ppermute | solution.py:19
  12.0 37.2 %copy-start.7 = (bf16[1024,200]{0,1:T(8,128)(2,1)S(1)}, bf16[1024,200]{0,1:T(8,128)(2,1)}, u32[]{:S(2)}) copy-start(bf16[1024,200]{0,1:T(8,128)(2,1)} %param.12) | copy-start | bytes 1228804
  12.0 37.9 %copy-start.1 = (bf16[200,1024]{1,0:T(8,128)(2,1)S(1)}, bf16[200,1024]{1,0:T(8,128)(2,1)}, u32[]{:S(2)}) copy-start(bf16[200,1024]{1,0:T(8,128)(2,1)} %get-tuple-element.9) | copy-start | bytes 1228804
  13.7 37.2 %copy-start.4 = (bf16[1600]{0:T(1024)(128)(2,1)S(1)}, bf16[1600]{0:T(1024)(128)(2,1)}, u32[]{:S(2)}) copy-start(bf16[1600]{0:T(1024)(128)(2,1)} %param.9) | copy-start | bytes 9604
  13.7 77.2 %copy-start.5 = (s32[512]{0:T(512)S(1)}, s32[512]{0:T(512)}, u32[]{:S(2)}) copy-start(s32[512]{0:T(512)} %param.14) | copy-start | bytes 6148
  13.7 78.2 %copy-start.6 = (f32[2,1024]{1,0:T(2,128)S(1)}, f32[2,1024]{1,0:T(2,128)}, u32[]{:S(2)}) copy-start(f32[2,1024]{1,0:T(2,128)} %param.11) | copy-start | bytes 24580
  49.2 0.7 collective-permute-start.2
  50.9 41.8 %collective-permute-start.1 = (bf16[1,1600]{1,0:T(2,128)(2,1)S(1)}, bf16[1,1600]{1,0:T(2,128)(2,1)S(1)}, u32[]{:S(2)}, u32[]{:S(2)}) collective-permute-start(bf16[1,1600]{1,0:T(2,128)(2,1)S(1)} %reshape.93), channel_id=1, source_target_pairs={{1,0},{0,1},{3,2},{2,3},{5,4},{4,5},{7,6},{6,7},{9,8},{8,9},{11,10... | collective-permute-start | bytes 9608 | tf_op jit(solution)/shard_map/ppermute | solution.py:19
  91.0 1.7 collective-permute-start.4
  166.5 4.3 %copy-start = (f32[512,1024]{1,0:T(8,128)S(1)}, f32[512,1024]{1,0:T(8,128)}, u32[]{:S(2)}) copy-start(f32[512,1024]{1,0:T(8,128)} %get-tuple-element.21) | copy-start | bytes 6291460
  168.5 2.2 collective-permute-start.5
  259.0 7.1 %copy-start.2 = (pred[512,640]{1,0:T(8,128)(4,1)S(1)}, pred[512,640]{1,0:T(8,128)(4,1)}, u32[]{:S(2)}) copy-start(pred[512,640]{1,0:T(8,128)(4,1)} %broadcast_compare_fusion) | copy-start | bytes 983044
  265.8 15.4 %collective-permute-start.3 = (bf16[128,1024]{1,0:T(8,128)(2,1)S(1)}, bf16[128,1024]{1,0:T(8,128)(2,1)S(1)}, u32[]{:S(2)}, u32[]{:S(2)}) collective-permute-start(bf16[128,1024]{1,0:T(8,128)(2,1)S(1)} %constant_dynamic-slice_fusion.1), channel_id=1, source_target_pairs={{0,2},{2,0},{4,6},{6,4},{8,10},{10,8},{12,14},{14,12},{16,18},{18,... | collective-permute-start | bytes 786440 | tf_op jit(solution)/shard_map/ppermute | solution.py:14
  282.2 7.2 %copy-start.3 = (s32[512,1]{0,1:T(1,128)S(1)}, s32[512,1]{0,1:T(1,128)}, u32[]{:S(2)}) copy-start(s32[512,1]{0,1:T(1,128)} %param.15) | copy-start | bytes 6148
  288.2 24.6 %collective-permute-start.6 = (bf16[512,1024]{0,1:T(8,128)(2,1)S(1)}, bf16[512,1024]{0,1:T(8,128)(2,1)S(1)}, u32[]{:S(2)}, u32[]{:S(2)}) collective-permute-start(bf16[512,1024]{0,1:T(8,128)(2,1)S(1)} %bitcast.67), channel_id=1, source_target_pairs={{1,0},{0,1},{3,2},{2,3},{5,4},{4,5},{7,6},{6,7},{9,8},{8,9},{11,10... | collective-permute-start | bytes 3145736 | tf_op jit(solution)/shard_map/ppermute | solution.py:19
  291.0 21.8 %copy-start.8 = (f32[1600]{0:T(1024)S(1)}, f32[1600]{0:T(1024)}, u32[]{:S(2)}) copy-start(f32[1600]{0:T(1024)} %param.13) | copy-start | bytes 19204
Sparse Core Ops, SparseCore 0:
  9.6 65.8 all-gather.7
  77.9 76.2 all-gather.9
  156.4 102.5 all-gather.5
